TPU v7x, 32 devices: a whole 2x2x4 slice. The times are simulated.
32 devices in a mesh: pipe: 2 (over core), dp: 16 (over z, y, x).
Axes of the slice: x: 2, y: 2, z: 4, core: 2. Of those that a mesh axis runs over, the one named last changes fastest.
Arguments:
- layer_input: bfloat16 [2, 16, 512, 768], P('pipe', 'dp'), may hold values from -100 to 100
- saved_qkv: bfloat16 [2, 16, 512, 2304], P('pipe', 'dp'), may hold values from -27 to 27
- ln_gain: float32 [2, 768], P('pipe'), may hold values from 0.1 to 1.9
- layer_weights: bfloat16 [2, 768, 3072], P('pipe', 'dp'), may hold values from -0.21875 to 0.21875
- rand_blocks: int32 [2, 12, 6, 3], P('pipe'), may hold values from 1 to 6, as said below
- out_grad: bfloat16 [16, 512, 768], P('dp'), may hold values from -6 to 6
Outputs:
- grad_inputs: bfloat16 [2, 16, 512, 768], P('pipe', 'dp')
- grad_weights: float32 [2, 768, 3072], P('pipe', 'dp')
Inputs may be any that keep to these rules, and one draw needn't show every extreme that they name: `rand_blocks`: for each layer, head and middle block i (entry i - 1), 3 different blocks other than i - 1, i and i + 1.
All inputs are finite; a program needn't handle non-finite values.
Results may differ from a plain program's by a relative error of at most 0.0072.
Values may be sent and summed in bfloat16 or wider, within the bound.
No kernel may reach another device: no remote copies, remote signals or barrier semaphores. Data moves between devices by JAX's collectives and lax.ppermute only.
A program may use at most 192 MiB of HBM per device.

v0:
```python
import jax
import jax.numpy as jnp
from jax import lax
from jax.sharding import PartitionSpec as P

HEADS = 12
HEAD_DIM = 64
BLOCK = 64


EPSILON = 1e-05
NEGATIVE = -1e30


def shifted(value, axis, steps):
    count = lax.axis_size(axis)
    leading, last = (max(0, -steps), min(count, count - steps))
    return lax.ppermute(value, axis, [(source, source + steps) for source in range(leading, last)])


def normalize(inputs, gain):
    values = inputs.astype(jnp.float32)
    centred = values - jnp.mean(values, axis=-1, keepdims=True)
    inverse_std = lax.rsqrt(jnp.mean(centred * centred, axis=-1, keepdims=True) + EPSILON)
    standard = centred * inverse_std
    return ((standard * gain).astype(jnp.bfloat16), standard, inverse_std)


def to_heads(matrix, block_count):
    return matrix.reshape(block_count, BLOCK, HEADS, HEAD_DIM).transpose(2, 0, 1, 3)


def from_heads(tiles):
    head_count, block_count, tile_rows, head_depth = tiles.shape
    return tiles.transpose(1, 2, 0, 3).reshape(block_count * tile_rows, head_count * head_depth)


def key_tables(random_rows):
    head_count, middle_count, draw_count = random_rows.shape
    block_count = middle_count + 2
    middle = jnp.arange(1, block_count - 1, dtype=jnp.int32)
    fixed_rows = jnp.stack(
        [
            jnp.zeros_like(middle),
            jnp.full_like(middle, block_count - 1),
            middle - 1,
            middle,
            middle + 1,
        ],
        axis=-1,
    )
    key_table = jnp.concatenate(
        [jnp.broadcast_to(fixed_rows, (head_count, middle_count, 5)), random_rows], axis=-1
    )
    always = middle >= 0
    edge_keep = jnp.stack([always, always, middle != 1, always, middle != block_count - 2], axis=-1)
    keep_mask = jnp.concatenate(
        [edge_keep, jnp.ones((middle_count, draw_count), dtype=jnp.bool_)], axis=-1
    )
    return (key_table, jnp.repeat(keep_mask, BLOCK, axis=-1))


def softmax_weights(scores):
    largest = jnp.max(scores, axis=-1, keepdims=True)
    powers = jnp.exp(scores - largest)
    return (powers / jnp.sum(powers, axis=-1, keepdims=True)).astype(jnp.bfloat16)


def product(form, left, right):
    return jnp.einsum(form, left, right, preferred_element_type=jnp.float32)


def arrange(projected, random_rows):
    length = projected.shape[0]
    block_count = length // BLOCK
    inner_width = HEADS * HEAD_DIM
    queries = to_heads(projected[:, :inner_width], block_count)
    keys_all = to_heads(projected[:, inner_width : 2 * inner_width], block_count)
    values_all = to_heads(projected[:, 2 * inner_width :], block_count)
    key_table, keep_mask = key_tables(random_rows)
    head_index = jnp.arange(HEADS)[:, None, None]
    slot_count = key_table.shape[-1]
    key_tiles = keys_all[head_index, key_table].reshape(
        HEADS, block_count - 2, slot_count * BLOCK, HEAD_DIM
    )
    value_tiles = values_all[head_index, key_table].reshape(
        HEADS, block_count - 2, slot_count * BLOCK, HEAD_DIM
    )
    middle_queries = queries[:, 1 : block_count - 1]
    global_queries = jnp.stack([queries[:, 0], queries[:, block_count - 1]], axis=1)
    flat_keys = keys_all.reshape(HEADS, length, HEAD_DIM)
    flat_values = values_all.reshape(HEADS, length, HEAD_DIM)
    return (
        queries,
        middle_queries,
        global_queries,
        key_tiles,
        value_tiles,
        flat_keys,
        flat_values,
        key_table,
        keep_mask,
    )


def softmax_part(arranged):
    (
        queries,
        middle_queries,
        global_queries,
        key_tiles,
        value_tiles,
        flat_keys,
        flat_values,
        key_table,
        keep_mask,
    ) = arranged
    score_scale = HEAD_DIM ** (-0.5)
    scores = product("hmqd,hmjd->hmqj", middle_queries, key_tiles) * score_scale
    scores = jnp.where(keep_mask[None, :, None, :], scores, NEGATIVE)
    middle_weights = softmax_weights(scores)
    global_weights = softmax_weights(
        product("hgqd,hjd->hgqj", global_queries, flat_keys) * score_scale
    )
    middle_out = product("hmqj,hmjd->hmqd", middle_weights, value_tiles)
    global_out = product("hgqj,hjd->hgqd", global_weights, flat_values)
    context = jnp.concatenate([global_out[:, :1], middle_out, global_out[:, 1:]], axis=1).astype(
        jnp.bfloat16
    )
    return (middle_weights, global_weights, context)


def attend_backward(grad_context, state):
    (
        queries,
        middle_queries,
        global_queries,
        key_tiles,
        value_tiles,
        flat_keys,
        flat_values,
        middle_weights,
        global_weights,
        context,
        key_table,
    ) = state
    block_count = queries.shape[1]
    score_scale = HEAD_DIM ** (-0.5)
    grad_tiles = to_heads(grad_context, block_count)
    row_delta = jnp.sum(grad_tiles.astype(jnp.float32) * context.astype(jnp.float32), axis=-1)
    middle_grad = grad_tiles[:, 1 : block_count - 1]
    middle_delta = row_delta[:, 1 : block_count - 1]
    weight_grad = product("hmqd,hmjd->hmqj", middle_grad, value_tiles)
    score_grad = (
        middle_weights.astype(jnp.float32) * (weight_grad - middle_delta[..., None])
    ).astype(jnp.bfloat16)
    query_middle = product("hmqj,hmjd->hmqd", score_grad, key_tiles) * score_scale
    key_slots = product("hmqj,hmqd->hmjd", score_grad, middle_queries) * score_scale
    value_slots = product("hmqj,hmqd->hmjd", middle_weights, middle_grad)
    slot_count = key_table.shape[-1]
    tile_shape = (HEADS, block_count - 2, slot_count, BLOCK, HEAD_DIM)
    head_index = jnp.arange(HEADS)[:, None, None]
    key_grad = (
        jnp.zeros(queries.shape, jnp.float32)
        .at[head_index, key_table]
        .add(key_slots.reshape(tile_shape))
    )
    value_grad = (
        jnp.zeros(queries.shape, jnp.float32)
        .at[head_index, key_table]
        .add(value_slots.reshape(tile_shape))
    )
    global_grad = jnp.stack([grad_tiles[:, 0], grad_tiles[:, block_count - 1]], axis=1)
    global_delta = jnp.stack([row_delta[:, 0], row_delta[:, block_count - 1]], axis=1)
    global_weight_grad = product("hgqd,hjd->hgqj", global_grad, flat_values)
    global_score_grad = (
        global_weights.astype(jnp.float32) * (global_weight_grad - global_delta[..., None])
    ).astype(jnp.bfloat16)
    query_global = product("hgqj,hjd->hgqd", global_score_grad, flat_keys) * score_scale
    key_grad = key_grad + (
        product("hgqj,hgqd->hjd", global_score_grad, global_queries) * score_scale
    ).reshape(queries.shape)
    value_grad = value_grad + product("hgqj,hgqd->hjd", global_weights, global_grad).reshape(
        queries.shape
    )
    query_grad = jnp.concatenate([query_global[:, :1], query_middle, query_global[:, 1:]], axis=1)
    return jnp.concatenate(
        [from_heads(query_grad), from_heads(key_grad), from_heads(value_grad)], axis=-1
    ).astype(jnp.bfloat16)


def layer_backward(upper_grad, standard, inverse_std, gain, weights_full, state):
    inner_width = HEADS * HEAD_DIM
    grad_context = jnp.dot(
        upper_grad, weights_full[:, 3 * inner_width :], preferred_element_type=jnp.float32
    ).astype(jnp.bfloat16)
    grad_projected = attend_backward(grad_context, state)
    grad_normed = lax.dot_general(
        grad_projected,
        weights_full[:, : 3 * inner_width],
        (((1,), (1,)), ((), ())),
        preferred_element_type=jnp.float32,
    )
    grad_standard = grad_normed * gain
    correction = jnp.mean(grad_standard, axis=-1, keepdims=True) + standard * jnp.mean(
        grad_standard * standard, axis=-1, keepdims=True
    )
    grad_input = (
        upper_grad.astype(jnp.float32) + inverse_std * (grad_standard - correction)
    ).astype(jnp.bfloat16)
    return (grad_input, grad_projected)


def cross_rows(left_cols, right_rows):
    return lax.dot_general(
        left_cols, right_rows, (((0,), (0,)), ((), ())), preferred_element_type=jnp.float32
    )


def forward_saved(layer_input, saved_qkv, gain, random_rows):
    normed, standard, inverse_std = normalize(layer_input[0, 0], gain)
    middle_weights, global_weights, context = softmax_part(arrange(saved_qkv[0, 0], random_rows))
    collected = [(normed, standard, inverse_std, middle_weights, global_weights, context)]
    return jax.tree.map(lambda *items: jnp.stack(items), *collected)


def run_chain(active_work, resting, out_grad, carry):
    section_index = lax.axis_index("pipe")
    sections = lax.axis_size("pipe")
    note_count = out_grad.shape[0]
    depth = sections - 1 - section_index
    received = jnp.zeros_like(out_grad[0])
    turn_count = sections + note_count - 1
    for turn_index in range(turn_count):
        note = turn_index - depth
        active = (note >= 0) & (note < note_count)
        safe_note = jnp.clip(note, 0, note_count - 1)
        top_grad = lax.dynamic_index_in_dim(out_grad, safe_note, 0, keepdims=False)
        upper_grad = jnp.where(depth == 0, top_grad, received)
        grad_input, carry = lax.cond(active, active_work, resting, upper_grad, safe_note, carry)
        if turn_index + 1 < turn_count:
            received = shifted(grad_input, "pipe", -1)
    return carry


def on_device(layer_input, saved_qkv, ln_gain, layer_weights, rand_blocks, out_grad):
    inner_width = HEADS * HEAD_DIM
    weights_full = lax.all_gather(layer_weights[0], "dp", axis=0, tiled=True)
    gain = ln_gain[0]
    random_rows = rand_blocks[0]
    note_count, length, width = out_grad.shape
    saved = forward_saved(layer_input, saved_qkv, gain, random_rows)

    def note_backward(upper_grad, note):
        normed, standard, inverse_std, middle_weights, global_weights, context = jax.tree.map(
            lambda item: lax.dynamic_index_in_dim(item, note, 0, keepdims=False), saved
        )
        note_projected = lax.dynamic_index_in_dim(saved_qkv[0], note, 0, keepdims=False)
        arranged = arrange(note_projected, random_rows)
        state = arranged[:7] + (middle_weights, global_weights, context, arranged[7])
        grad_input, grad_projected = layer_backward(
            upper_grad, standard, inverse_std, gain, weights_full, state
        )
        return (grad_input, grad_projected, normed, context)

    def store(old_value, fresh_value, note):
        return lax.dynamic_update_index_in_dim(old_value, fresh_value, note, 0)

    def resting(upper_grad, note, carry):
        return (jnp.zeros_like(upper_grad), carry)

    def active_work(upper_grad, note, carry):
        grad_store, projected_kept, upper_kept = carry
        grad_input, grad_projected, normed, context = note_backward(upper_grad, note)
        return (
            grad_input,
            (
                store(grad_store, grad_input, note),
                store(projected_kept, grad_projected, note),
                store(upper_kept, upper_grad, note),
            ),
        )

    start_carry = (
        jnp.zeros_like(out_grad),
        jnp.zeros((note_count, length, 3 * inner_width), jnp.bfloat16),
        jnp.zeros_like(out_grad),
    )
    grad_input, projected_kept, upper_kept = run_chain(active_work, resting, out_grad, start_carry)
    normed_all = saved[0]
    context_all = saved[5]
    normed_cols = normed_all[0]
    upper_cols = upper_kept[0]
    term = jnp.concatenate(
        [
            cross_rows(normed_cols, projected_kept[0]),
            cross_rows(upper_cols, from_heads(context_all[0])),
        ],
        axis=1,
    )
    summed = lax.psum_scatter(term, "dp", scatter_dimension=0, tiled=True)
    scaled = summed / lax.axis_size("dp")
    return (grad_input[None], scaled[None])


def solution(mesh):
    placed = (
        P("pipe", "dp", None, None),
        P("pipe", "dp", None, None),
        P("pipe", None),
        P("pipe", "dp", None),
        P("pipe", None, None, None),
        P("dp", None, None),
    )
    return jax.shard_map(
        on_device,
        mesh=mesh,
        in_specs=placed,
        out_specs=(P("pipe", "dp", None, None), P("pipe", "dp", None)),
        check_vma=False,
    )
```

profile of v0, /device:TPU:0, one launch (start us, length us, event | category | flops | bytes accessed | tf_op | source)
XLA Modules:
  0.0 877.5 jit_solution(6692606181873471050)
XLA Ops:
  9.7 2.2 reshape.819
  15.2 2.2 reshape.818
  17.4 3.2 copy.226
  21.0 2.2 reshape.820
  25.2 10.0 %gather_fusion.4 = bf16[576,64,64]{2,1,0:T(8,128)(2,1)} fusion(bf16[12,8,64,64]{3,2,1,0:T(8,128)(2,1)S(1)} %bitcast.327, s32[576]{0:T(1024)S(1)} %reshape.751), kind=kCustom, calls=%fused_computation.4 | custom fusion | bytes 9441792 | tf_op jit(solution)/shard_map/gather | solution.py:83
  35.2 10.0 %gather_fusion.5 = bf16[576,64,64]{2,1,0:T(8,128)(2,1)} fusion(bf16[12,8,64,64]{3,2,1,0:T(8,128)(2,1)S(1)} %bitcast.328, s32[576]{0:T(1024)S(1)} %reshape.751), kind=kCustom, calls=%fused_computation.5 | custom fusion | bytes 9441792 | tf_op jit(solution)/shard_map/gather | solution.py:86
  46.4 2.7 fusion.108
  49.2 4.5 fusion.149
  56.7 5.8 fusion.111
  62.5 10.2 %fusion.150 = (f32[12,6,64]{2,1,0:T(8,128)S(1)}, f32[12,6,64,512]{3,2,1,0:T(8,128)S(1)}) fusion(f32[12,6,512,64]{2,3,1,0:T(8,128)} %fusion.111, pred[6,512]{1,0:T(8,128)(4,1)S(1)} %broadcast_in_dim.82), kind=kOutput, calls=%fused_computation.225 | output fusion | flops 14156287 | bytes 18895872 | tf_op jit(solution)/shard_map/sub | solution.py:65
  72.7 5.5 convolution_convert_fusion.2
  82.6 2.7 fusion.133
  85.3 8.7 all-gather.3.cloned.1.call-done
  94.0 14.4 %conditional.2 = (bf16[512,768]{1,0:T(8,128)(2,1)}, bf16[1,512,768]{2,1,0:T(8,128)(2,1)}, bf16[1,512,2304]{1,2,0:T(8,128)(2,1)}, bf16[1,512,768]{2,1,0:T(8,128)(2,1)}) conditional(s32[]{:T(128)} %convert_element_type.152, () %tuple.37, (pred[]{:T(512)}, bf16[512,768]{1,0:T(8,128)(2,1)S(1)}, f32[1,512,1]{1,2,0:T(1,128)S(1)}, ...), branch_computations={%region_6.7_spmd, %region_7.13_spmd} | conditional | flops 4071164672 | bytes 320970560 | solution.py:240
  111.0 2.9 maximum_bitcast_fusion.1
  113.9 2.9 copy.146
  116.8 3.5 reshape.723
  120.3 272.3 %collective-permute-done = bf16[512,768]{1,0:T(8,128)(2,1)S(1)} collective-permute-done((bf16[512,768]{1,0:T(8,128)(2,1)}, bf16[512,768]{1,0:T(8,128)(2,1)S(1)}, u32[]{:S(2)}, u32[]{:S(2)}) %collective-permute-start) | collective-permute-done | bytes 786464 | tf_op jit(solution)/shard_map/ppermute | solution.py:18
  392.6 287.6 %conditional.3 = (bf16[1,1,512,768]{3,2,1,0:T(8,128)(2,1)}, bf16[512,2304]{0,1:T(8,128)(2,1)}, bf16[512,768]{1,0:T(8,128)(2,1)}) conditional(s32[]{:T(128)} %convert_element_type.151, (bf16[1,512,768]{2,1,0:T(8,128)(2,1)}, bf16[1,512,2304]{1,2,0:T(8,128)(2,1)}, bf16[1,512,768]{2,1,0:T(8,128)(2,1)}) %tuple.82, (pred[]{:T(512)}, ...), branch_computations={%region_13.14_spmd, %region_14.20_spmd} | conditional | flops 4056222464 | bytes 290290720 | solution.py:240
  393.7 2.3 convolution_convert_fusion.1
  396.0 2.2 reshape.813
  398.2 3.2 fusion.55
  402.0 4.3 copy.145
  406.4 3.1 fusion.141
  409.5 3.2 reshape.694
  412.6 3.5 reshape.802
  416.1 2.9 multiply_convert_fusion.3
  419.0 2.4 reshape.696
  423.2 2.2 fusion.70
  427.8 2.1 copy.108
  429.9 10.0 %gather_fusion.2 = bf16[576,64,64]{2,1,0:T(8,128)(2,1)} fusion(bf16[12,8,64,64]{3,2,1,0:T(8,128)(2,1)S(1)} %bitcast.332, s32[576]{0:T(1024)S(1)} %reshape.739), kind=kCustom, calls=%fused_computation.2 | custom fusion | bytes 9441792 | tf_op jit(solution)/shard_map/cond/branch_1_fun/gather | solution.py:86
  440.7 12.6 %multiply_convert_fusion.2 = bf16[12,6,64,512]{3,2,1,0:T(8,128)(2,1)} fusion(bf16[1,12,6,64,512]{4,3,2,1,0:T(8,128)(2,1)} %get-tuple-element.153, f32[12,6,64]{2,1,0:T(8,128)S(1)} %slice.218, bf16[12,8,64,64]{3,2,1,0:T(8,128)(2,1)S(1)} %get-tuple-element.249, bf16[12,6,512,64]{3,2,1,0:T(8,128)(2,1)} %bitcast.354), kind=kOutput, calls=%fused_computation.78 | convolution fusion | flops 311427072 | bytes 14960640 | tf_op jit(solution)/shard_map/cond/branch_1_fun/hmqd,hmjd->hmqj/dot_general | solution.py:70
  455.4 10.2 %gather_fusion.3 = bf16[576,64,64]{2,1,0:T(8,128)(2,1)} fusion(bf16[12,8,64,64]{3,2,1,0:T(8,128)(2,1)S(1)} %bitcast.330, s32[576]{0:T(1024)S(1)} %reshape.739), kind=kCustom, calls=%fused_computation.3 | custom fusion | bytes 9441792 | tf_op jit(solution)/shard_map/cond/branch_1_fun/gather | solution.py:83
  465.6 6.9 multiply_convert_fusion.4
  475.9 2.4 reshape.701
  483.7 7.7 broadcast_multiply_fusion.3
  491.4 13.8 %copy.184 = f32[12,6,512,64]{3,2,1,0:T(8,128)} copy(f32[12,6,512,64]{2,3,1,0:T(8,128)} %broadcast_multiply_fusion.3) | data formatting | bytes 18874368 | tf_op jit(solution)/shard_map/cond/branch_1_fun/reshape | solution.py:166
  506.1 63.1 %scatter_fusion.2 = f32[12,8,64,64]{3,2,1,0:T(8,128)S(1)} fusion(f32[12,8,64,64]{3,2,1,0:T(8,128)S(1)} %bitcast.324, s32[576]{0:T(1024)S(1)} %reshape.775, f32[576,64,64]{2,1,0:T(8,128)} %bitcast.334), kind=kCustom, calls=%fused_computation.8 | custom fusion | flops 2359296 | bytes 28316160 | tf_op jit(solution)/shard_map/cond/branch_1_fun/scatter-add | solution.py:166
  580.2 7.8 fusion.52
  588.0 13.8 %copy.186 = f32[12,6,512,64]{3,2,1,0:T(8,128)} copy(f32[12,6,512,64]{2,3,1,0:T(8,128)} %fusion.52) | data formatting | bytes 18874368 | tf_op jit(solution)/shard_map/cond/branch_1_fun/reshape | solution.py:171
  601.8 63.1 %scatter_fusion.3 = f32[12,8,64,64]{3,2,1,0:T(8,128)S(1)} fusion(f32[12,8,64,64]{3,2,1,0:T(8,128)S(1)} %bitcast.326, s32[576]{0:T(1024)S(1)} %reshape.775, f32[576,64,64]{2,1,0:T(8,128)} %bitcast.336), kind=kCustom, calls=%fused_computation.9 | custom fusion | flops 2359296 | bytes 28316160 | tf_op jit(solution)/shard_map/cond/branch_1_fun/scatter-add | solution.py:171
  666.4 2.2 copy.127
  670.4 2.1 constant_dynamic-update-slice_fusion
  672.6 4.9 fusion.135
  677.5 2.4 fusion.73
  680.2 7.1 fusion.114
  689.3 8.0 pad_maximum_fusion.9
  697.4 170.9 %reduce-scatter.2.cloned.1.call-done = f32[48,3072]{1,0:T(8,128)} async-done(((f32[768,3072]{1,0:T(8,128)}), f32[48,3072]{1,0:T(8,128)}) %reduce-scatter.2.cloned.1.call-update) | async-done | bytes 589840 | tf_op jit(solution)/shard_map/reduce_scatter | solution.py:301
  (140 shorter events, 59.8 us)
Async XLA Ops:
  7.2 86.8 %all-gather.3.cloned.1.call-start = ((), (), s32[]{:S(2)}) async-start(), calls=%async_computation.2 | async-start | bytes 5013504 | tf_op jit(solution)/shard_map/all_gather | solution.py:248
  7.9 860.3 %reduce-scatter.2.cloned.1.call-start = ((), (), s32[]{:S(2)}) async-start(), calls=%async_computation.1 | async-start | bytes 10027008 | tf_op jit(solution)/shard_map/reduce_scatter | solution.py:301
  12.0 2.0 copy-start.41
  35.2 10.0 %copy-start.22 = (bf16[1,1,512,768]{3,2,1,0:T(8,128)(2,1)S(1)}, bf16[1,1,512,768]{3,2,1,0:T(8,128)(2,1)}, u32[]{:S(2)}) copy-start(bf16[1,1,512,768]{3,2,1,0:T(8,128)(2,1)} %param.10) | copy-start | bytes 2359300
  46.4 9.0 %slice-start = ((s8[9437184]{0:T(1024)(128)(4,1)}), s8[4194304]{0:T(1024)(128)(4,1)S(1)}, s32[]{:S(2)}) async-start(s8[9437184]{0:T(1024)(128)(4,1)} %bitcast.339), calls=%async_computation.3 | async-start | bytes 8388608
  49.1 4.5 copy-start.21
  49.2 6.3 slice-start.1
  53.7 1.7 copy-start.17
  53.7 2.0 slice-start.2
  53.7 3.0 copy-start.27
  55.4 22.8 %copy-start.32 = (bf16[12,1,64,64]{3,2,1,0:T(8,128)(2,1)}, bf16[12,1,64,64]{3,2,1,0:T(8,128)(2,1)S(1)}, u32[]{:S(2)}) copy-start(bf16[12,1,64,64]{3,2,1,0:T(8,128)(2,1)S(1)} %get-tuple-element.287) | copy-start | bytes 294916
  55.4 22.8 %copy-start.33 = (bf16[12,1,64,64]{3,2,1,0:T(8,128)(2,1)}, bf16[12,1,64,64]{3,2,1,0:T(8,128)(2,1)S(1)}, u32[]{:S(2)}) copy-start(bf16[12,1,64,64]{3,2,1,0:T(8,128)(2,1)S(1)} %get-tuple-element.288) | copy-start | bytes 294916
  78.2 3.4 copy-start.30
  79.8 2.5 copy-start.18
  79.8 2.8 copy-start.48
  80.2 13.8 %copy-start.42 = (f32[512]{0:T(512)}, f32[512]{0:T(512)S(1)}, u32[]{:S(2)}) copy-start(f32[512]{0:T(512)S(1)} %add_rsqrt_fusion) | copy-start | bytes 6148
  82.6 11.4 %copy-start = (bf16[1,12,2,64,512]{4,3,2,1,0:T(8,128)(2,1)}, bf16[1,12,2,64,512]{4,3,2,1,0:T(8,128)(2,1)S(1)}, u32[]{:S(2)}) copy-start(bf16[1,12,2,64,512]{4,3,2,1,0:T(8,128)(2,1)S(1)} %fusion.132) | copy-start | bytes 4718596
  82.6 11.4 %copy-start.23 = (bf16[1,512,768]{2,1,0:T(8,128)(2,1)S(1)}, bf16[1,512,768]{2,1,0:T(8,128)(2,1)}, u32[]{:S(2)}) copy-start(bf16[1,512,768]{2,1,0:T(8,128)(2,1)} %param.15) | copy-start | bytes 2359300
  108.4 284.3 %collective-permute-start = (bf16[512,768]{1,0:T(8,128)(2,1)}, bf16[512,768]{1,0:T(8,128)(2,1)S(1)}, u32[]{:S(2)}, u32[]{:S(2)}) collective-permute-start(bf16[512,768]{1,0:T(8,128)(2,1)} %get-tuple-element.169), channel_id=1, source_target_pairs={{16,0},{17,1},{18,2},{19,3},{20,4},{21,5},{22,6},{23,7},{24,8},{25... | collective-permute-start | bytes 2359304 | tf_op jit(solution)/shard_map/ppermute | solution.py:18
  113.9 278.7 %copy-start.1 = (bf16[1,12,2,64,512]{4,3,2,1,0:T(8,128)(2,1)S(1)}, bf16[1,12,2,64,512]{4,3,2,1,0:T(8,128)(2,1)}, u32[]{:S(2)}) copy-start(bf16[1,12,2,64,512]{4,3,2,1,0:T(8,128)(2,1)} %copy-done) | copy-start | bytes 4718596
  113.9 278.7 %copy-start.24 = (bf16[1,512,768]{2,1,0:T(8,128)(2,1)S(1)}, bf16[1,512,768]{2,1,0:T(8,128)(2,1)}, u32[]{:S(2)}) copy-start(bf16[1,512,768]{2,1,0:T(8,128)(2,1)} %param.15) | copy-start | bytes 2359300
  392.6 23.5 %copy-start.4 = (bf16[1,12,2,64,512]{4,3,2,1,0:T(8,128)(2,1)}, bf16[1,12,2,64,512]{4,3,2,1,0:T(8,128)(2,1)S(1)}, u32[]{:S(2)}) copy-start(bf16[1,12,2,64,512]{4,3,2,1,0:T(8,128)(2,1)S(1)} %get-tuple-element.149) | copy-start | bytes 4718596 | tf_op jit(solution)/shard_map/cond
  401.4 0.6 copy-start.40
  401.4 39.3 %copy-start.6 = (bf16[12,8,64,64]{3,2,1,0:T(8,128)(2,1)}, bf16[12,8,64,64]{3,2,1,0:T(8,128)(2,1)S(1)}, u32[]{:S(2)}) copy-start(bf16[12,8,64,64]{3,2,1,0:T(8,128)(2,1)S(1)} %get-tuple-element.249) | copy-start | bytes 2359300 | tf_op jit(solution)/shard_map/cond
  421.4 3.9 copy-start.13
  465.6 7.0 copy-start.36
  465.6 7.0 copy-start.37
  478.3 1.6 copy-start.28
  478.8 1.2 copy-start.20
  572.7 3.8 copy-start.5
  668.7 3.8 copy-start.47
  668.7 3.8 copy-start.9
  672.6 4.9 copy-start.45
  680.2 7.1 copy-start.31
Sparse Core Ops, SparseCore 0:
  10.8 83.1 all-gather.2
  697.5 170.6 reduce-scatter.1
where the time goes:
time: 890 us; the launch traced here: 877 us
  waiting for transfers between devices  453 us (51%)
  other arithmetic  173 us (19%)
  local copies, waits for them, and re-layouts  150 us (17%)
  matrix products  74.7 us (8%)
  between operations  14.9 us (2%)
  loops' own time  10.6 us (1%)
    ppermute x1, waiting for transfers between devices, shifted(): lax.ppermute(value, axis, [(source, source + steps) for source in range(l...  272 us
    reduce_scatter x1, waiting for transfers between devices, on_device(): summed = lax.psum_scatter(term, 'dp', scatter_dimension=0, tiled=True)  171 us
    scatter-add x1, other arithmetic, attend_backward(): key_grad = jnp.zeros(queries.shape, jnp.float32).at[head_index, key_table...  63.1 us
    scatter-add x1, other arithmetic, attend_backward(): value_grad = jnp.zeros(queries.shape, jnp.float32).at[head_index, key_tab...  63.1 us
    dot_general x12, matrix products, product(): return jnp.einsum(form, left, right, preferred_element_type=jnp.float32)  58.5 us
    reshape x13, local copies, waits for them, and re-layouts, to_heads(): matrix.reshape(block_count, BLOCK, HEADS, HEAD_DIM).transpose(2, 0, 1, 3)  28.9 us
    gather x2, local copies, waits for them, and re-layouts, arrange(): keys_all[head_index, key_table]  20.2 us
    gather x2, local copies, waits for them, and re-layouts, arrange(): values_all[head_index, key_table]  20 us
  transfers between devices with their start and end apart: 3, of which 3 were waited for; matrix products, arithmetic and copies ran while one was open for 10% of the time, Pallas kernels for 0%

commit v1 on v0

v1 whole, which is shorter than its diff:
```python
import math

import jax
import jax.numpy as jnp
from jax import lax
from jax.experimental import pallas as pl
from jax.experimental.pallas import tpu as pltpu
from jax.sharding import PartitionSpec as P

HEADS = 12
HEAD_DIM = 64
BLOCK = 64
INNER = HEADS * HEAD_DIM
PAIR = 2 * HEAD_DIM
PAIRS = HEADS // 2
EPSILON = 1e-05
NEGATIVE = -1e30
SCALE = HEAD_DIM ** (-0.5)
VMEM_LIMIT = 60 * 1024 * 1024
F32 = jnp.float32
BF16 = jnp.bfloat16
ANY = pl.BlockSpec(memory_space=pl.ANY)
SMEM = pl.BlockSpec(memory_space=pltpu.SMEM)


def dot_nn(left, right):
    return lax.dot_general(left, right, (((1,), (0,)), ((), ())), preferred_element_type=F32)


def dot_nt(left, right):
    return lax.dot_general(left, right, (((1,), (1,)), ((), ())), preferred_element_type=F32)


def dot_tn(left, right):
    return lax.dot_general(left, right, (((0,), (0,)), ((), ())), preferred_element_type=F32)


def call(body, out_shape, in_specs, out_specs, scratch, aliases=None):
    return pl.pallas_call(
        body,
        out_shape=out_shape,
        in_specs=in_specs,
        out_specs=out_specs,
        scratch_shapes=scratch,
        input_output_aliases=aliases or {},
        compiler_params=pltpu.CompilerParams(vmem_limit_bytes=VMEM_LIMIT),
    )


def shape(dims, dtype=BF16):
    return jax.ShapeDtypeStruct(dims, dtype)


def scaled(value):
    return (value.astype(F32) * SCALE).astype(BF16)


def forward_body(skip_ref, q_ref, k_ref, v_ref, weights_ref, context_ref):
    pair = pl.program_id(0)
    length = q_ref.shape[0]
    last = length // BLOCK - 1
    queries = scaled(q_ref[...])
    keys = k_ref[...]
    values_t = v_ref[...].T
    lane = lax.broadcasted_iota(jnp.int32, keys.shape, 1)
    key_block = lax.broadcasted_iota(jnp.int32, (length, length), 0) // BLOCK
    query_block = lax.broadcasted_iota(jnp.int32, (length, length), 1) // BLOCK
    parts = []
    for half in range(2):
        own = (lane >= half * HEAD_DIM) & (lane < (half + 1) * HEAD_DIM)
        scores = dot_nt(jnp.where(own, keys, jnp.zeros_like(keys)), queries)
        low = skip_ref[0, 2 * pair + half]
        high = skip_ref[1, 2 * pair + half]
        masked = ((query_block == 1) & (key_block == low)) | (
            (query_block == last - 1) & (key_block == high)
        )
        scores = jnp.where(masked, NEGATIVE, scores)
        powers = jnp.exp(scores - jnp.max(scores, axis=0, keepdims=True))
        inverse = 1.0 / jnp.sum(powers, axis=0, keepdims=True)
        weights = (powers * inverse).astype(BF16)
        weights_ref[half] = weights
        parts.append(dot_nn(values_t[half * HEAD_DIM : (half + 1) * HEAD_DIM], weights))
    context_ref[...] = jnp.concatenate(parts, axis=0).T.astype(BF16)


def attend_forward(projected, skipped):
    length = projected.shape[0]
    block = (length, PAIR)
    return pl.pallas_call(
        forward_body,
        grid_spec=pltpu.PrefetchScalarGridSpec(
            num_scalar_prefetch=1,
            grid=(PAIRS,),
            in_specs=[
                pl.BlockSpec(block, lambda p, s: (0, p)),
                pl.BlockSpec(block, lambda p, s: (0, PAIRS + p)),
                pl.BlockSpec(block, lambda p, s: (0, 2 * PAIRS + p)),
            ],
            out_specs=[
                pl.BlockSpec((2, length, length), lambda p, s: (p, 0, 0)),
                pl.BlockSpec(block, lambda p, s: (0, p)),
            ],
        ),
        out_shape=(shape((HEADS, length, length)), shape((length, INNER))),
        compiler_params=pltpu.CompilerParams(vmem_limit_bytes=VMEM_LIMIT),
    )(skipped, projected, projected, projected)


def statistics(x):
    values = x.astype(F32)
    centred = values - jnp.mean(values, axis=-1, keepdims=True)
    inverse = lax.rsqrt(jnp.mean(centred * centred, axis=-1, keepdims=True) + EPSILON)
    return centred * inverse, inverse


def norm_body(x_ref, gain_ref, out_ref):
    standard, _ = statistics(x_ref[...])
    out_ref[...] = (standard * gain_ref[...]).astype(BF16).T


def normed_transposed(x, gain):
    length, width = x.shape
    return pl.pallas_call(norm_body, out_shape=shape((width, length)))(x, gain)


def weight_copies(info_ref, pieces, offsets, columns, target, sems, wanted):
    low, high = wanted
    copies = []
    for (first, second), order, (start, stop) in zip(pieces, offsets, columns):
        left, right = max(start, low), min(stop, high)
        if left >= right:
            continue
        half = first.shape[0]
        rows = first.shape[1]
        for slot, offset in enumerate(order):
            source = first if slot < half else second
            row = pl.multiple_of((info_ref[2] ^ offset) * rows, math.gcd(rows, 16))
            copies.append(
                pltpu.make_async_copy(
                    source.at[slot % half, :, pl.ds(left - start, right - left)],
                    target.at[pl.ds(row, rows), pl.ds(left - low, right - left)],
                    sems.at[len(copies)],
                )
            )
    return copies


def attend_body(offsets, columns, aliased, *refs):
    info_ref, received, top, qkv, weights, context = refs[:6]
    chunk_count = len(columns)
    pieces = [(refs[6 + 2 * c], refs[7 + 2 * c]) for c in range(chunk_count)]
    refs = refs[6 + 2 * chunk_count + aliased :]
    grad_out, upper_out = refs[:2]
    upper_v, qkv_v, p_v, context_v, out_w, gc_v, grad_v, base_sems, p_sems, w_sems = refs[2:]

    @pl.when(info_ref[0] == 1)
    def _():
        upper_top = pltpu.make_async_copy(top, upper_v, base_sems.at[0])
        upper_got = pltpu.make_async_copy(received, upper_v, base_sems.at[1])

        @pl.when(info_ref[1] == 1)
        def _():
            upper_top.start()

        @pl.when(info_ref[1] == 0)
        def _():
            upper_got.start()

        w_copies = weight_copies(
            info_ref, pieces, offsets, columns, out_w, w_sems, (3 * INNER, 4 * INNER)
        )
        for copy in w_copies:
            copy.start()
        qkv_copy = pltpu.make_async_copy(qkv, qkv_v, base_sems.at[2])
        context_copy = pltpu.make_async_copy(context, context_v, base_sems.at[3])
        qkv_copy.start()
        context_copy.start()

        def p_copy(pair):
            part = pl.ds(2 * pair, 2)
            return pltpu.make_async_copy(weights.at[part], p_v.at[part], p_sems.at[pair])

        for pair in range(PAIRS):
            p_copy(pair).start()

        @pl.when(info_ref[1] == 1)
        def _():
            upper_top.wait()

        @pl.when(info_ref[1] == 0)
        def _():
            upper_got.wait()

        upper_copy = pltpu.make_async_copy(upper_v, upper_out, base_sems.at[4])
        upper_copy.start()
        for copy in w_copies:
            copy.wait()
        gc_v[...] = dot_nn(upper_v[...], out_w[...]).astype(BF16)
        qkv_copy.wait()
        context_copy.wait()

        def one_pair(pair, carry):
            p_copy(pair).wait()
            base = pl.multiple_of(pair * PAIR, PAIR)
            at = pl.ds(base, PAIR)
            k_at = pl.ds(pl.multiple_of(base + INNER, PAIR), PAIR)
            v_at = pl.ds(pl.multiple_of(base + 2 * INNER, PAIR), PAIR)
            queries = scaled(qkv_v[:, at])
            keys_t = scaled(qkv_v[:, k_at]).T
            values = qkv_v[:, v_at]
            grads = gc_v[:, at]
            lane = lax.broadcasted_iota(jnp.int32, grads.shape, 1)
            zero = jnp.zeros_like(grads)
            product_t = (grads.astype(F32) * context_v[:, at].astype(F32)).T
            key_grad = value_grad = None
            query_parts = []
            for half in range(2):
                rows = slice(half * HEAD_DIM, (half + 1) * HEAD_DIM)
                own = (lane >= half * HEAD_DIM) & (lane < (half + 1) * HEAD_DIM)
                probs = p_v[2 * pair + half]
                delta = jnp.sum(product_t[rows], axis=0, keepdims=True)
                weight_grad = dot_nt(jnp.where(own, values, zero), grads)
                score_grad = (probs.astype(F32) * (weight_grad - delta)).astype(BF16)
                key_part = dot_nn(score_grad, jnp.where(own, queries, zero))
                value_part = dot_nn(probs, jnp.where(own, grads, zero))
                key_grad = key_part if half == 0 else key_grad + key_part
                value_grad = value_part if half == 0 else value_grad + value_part
                query_parts.append(dot_nn(keys_t[rows], score_grad))
            grad_v[:, at] = jnp.concatenate(query_parts, axis=0).T.astype(BF16)
            grad_v[:, k_at] = key_grad.astype(BF16)
            grad_v[:, v_at] = value_grad.astype(BF16)
            return carry

        lax.fori_loop(0, PAIRS, one_pair, 0)
        grad_copy = pltpu.make_async_copy(grad_v, grad_out, base_sems.at[5])
        grad_copy.start()
        upper_copy.wait()
        grad_copy.wait()


def attend_backward(info, received, top, qkv, weights, context, gathered, layout, carry):
    offsets, columns = layout
    length, width = top.shape
    flat = [piece for pair in gathered for piece in pair]
    inputs = [info, received, top, qkv, weights, context] + flat
    aliases = {}
    if carry is not None:
        aliases = {len(inputs): 0, len(inputs) + 1: 1}
        inputs = inputs + list(carry)
    copies = sum(
        len(order) for order, (start, stop) in zip(offsets, columns) if stop > 3 * INNER
    )

    def body(*refs):
        attend_body(offsets, columns, len(aliases), *refs)

    return call(
        body,
        (shape((length, 3 * INNER)), shape((length, width))),
        [SMEM] + [ANY] * (len(inputs) - 1),
        (ANY, ANY),
        [
            pltpu.VMEM((length, width), BF16),
            pltpu.VMEM((length, 3 * INNER), BF16),
            pltpu.VMEM((HEADS, length, length), BF16),
            pltpu.VMEM((length, INNER), BF16),
            pltpu.VMEM((width, INNER), BF16),
            pltpu.VMEM((length, INNER), BF16),
            pltpu.VMEM((length, 3 * INNER), BF16),
            pltpu.SemaphoreType.DMA((6,)),
            pltpu.SemaphoreType.DMA((PAIRS,)),
            pltpu.SemaphoreType.DMA((copies,)),
        ],
        aliases,
    )(*inputs)


def project_body(offsets, columns, aliased, *refs):
    info_ref, gain_ref, upper, grad, x = refs[:5]
    chunk_count = len(columns)
    pieces = [(refs[5 + 2 * c], refs[6 + 2 * c]) for c in range(chunk_count)]
    refs = refs[5 + 2 * chunk_count + aliased :]
    out = refs[0]
    upper_v, grad_v, x_v, w_v, out_v, sems, w_sems = refs[1:]

    @pl.when(info_ref[0] == 1)
    def _():
        copies = weight_copies(info_ref, pieces, offsets, columns, w_v, w_sems, (0, 3 * INNER))
        for index, (source, target) in enumerate(((upper, upper_v), (grad, grad_v), (x, x_v))):
            copies.append(pltpu.make_async_copy(source, target, sems.at[index]))
        for copy in copies:
            copy.start()
        for copy in copies:
            copy.wait()
        grad_standard = dot_nt(grad_v[...], w_v[...]) * gain_ref[...]
        standard, inverse = statistics(x_v[...])
        correction = jnp.mean(grad_standard, axis=-1, keepdims=True) + standard * jnp.mean(
            grad_standard * standard, axis=-1, keepdims=True
        )
        out_v[...] = (
            upper_v[...].astype(F32) + inverse * (grad_standard - correction)
        ).astype(BF16)
        done = pltpu.make_async_copy(out_v, out, sems.at[3])
        done.start()
        done.wait()


def project(info, gain, upper, grad, x, gathered, layout, carry):
    offsets, columns = layout
    length, width = x.shape
    flat = [piece for pair in gathered for piece in pair]
    inputs = [info, gain, upper, grad, x] + flat
    aliases = {}
    if carry is not None:
        aliases = {len(inputs): 0}
        inputs = inputs + [carry]
    copies = sum(
        len(order) for order, (start, stop) in zip(offsets, columns) if start < 3 * INNER
    )

    def body(*refs):
        project_body(offsets, columns, len(aliases), *refs)

    return call(
        body,
        shape((length, width)),
        [SMEM, pl.BlockSpec(memory_space=pltpu.VMEM)] + [ANY] * (len(inputs) - 2),
        ANY,
        [
            pltpu.VMEM((length, width), BF16),
            pltpu.VMEM((length, 3 * INNER), BF16),
            pltpu.VMEM((length, width), BF16),
            pltpu.VMEM((width, 3 * INNER), BF16),
            pltpu.VMEM((length, width), BF16),
            pltpu.SemaphoreType.DMA((4,)),
            pltpu.SemaphoreType.DMA((copies,)),
        ],
        aliases,
    )(*inputs)


def term_body(offsets, columns, *refs):
    info_ref, normed_t, grad, upper, context = refs[:5]
    outs = refs[5 : 5 + 2 * len(columns)]
    normed_v, grad_v, upper_v, context_v, term_v, sems, out_sems = refs[5 + 2 * len(columns) :]
    loads = [
        pltpu.make_async_copy(source, target, sems.at[index])
        for index, (source, target) in enumerate(
            ((normed_t, normed_v), (grad, grad_v), (upper, upper_v), (context, context_v))
        )
    ]
    for load in loads:
        load.start()
    copies = []

    def send(low, high):
        for chunk, ((start, stop), order) in enumerate(zip(columns, offsets)):
            left, right = max(start, low), min(stop, high)
            if left >= right:
                continue
            half = outs[2 * chunk].shape[0]
            rows = outs[2 * chunk].shape[1]
            for slot, offset in enumerate(order):
                target = outs[2 * chunk + (slot >= half)]
                row = pl.multiple_of((info_ref[2] ^ offset) * rows, math.gcd(rows, 16))
                copy = pltpu.make_async_copy(
                    term_v.at[pl.ds(row, rows), pl.ds(left, right - left)],
                    target.at[slot % half, :, pl.ds(left - start, right - left)],
                    out_sems.at[len(copies)],
                )
                copy.start()
                copies.append(copy)

    loads[0].wait()
    loads[1].wait()
    for group in range(3):
        low = group * INNER
        term_v[:, low : low + INNER] = dot_nn(
            normed_v[...], grad_v[:, low : low + INNER]
        ).astype(BF16)
        send(low, low + INNER)
    loads[2].wait()
    loads[3].wait()
    term_v[:, 3 * INNER :] = dot_tn(upper_v[...], context_v[...]).astype(BF16)
    send(3 * INNER, 4 * INNER)
    for copy in copies:
        copy.wait()


def weight_terms(info, normed_t, grad, upper, context, rows, layout):
    offsets, columns = layout
    width, length = normed_t.shape
    count = len(offsets[0])
    outs = tuple(
        shape((count // 2, rows, stop - start)) for start, stop in columns for _ in range(2)
    )
    copies = 0
    for group in range(4):
        for order, (start, stop) in zip(offsets, columns):
            if max(start, group * INNER) < min(stop, (group + 1) * INNER):
                copies += len(order)

    def body(*refs):
        term_body(offsets, columns, *refs)

    return call(
        body,
        outs,
        [SMEM] + [ANY] * 4,
        (ANY,) * len(outs),
        [
            pltpu.VMEM((width, length), BF16),
            pltpu.VMEM((length, 3 * INNER), BF16),
            pltpu.VMEM((length, width), BF16),
            pltpu.VMEM((length, INNER), BF16),
            pltpu.VMEM((width, 4 * INNER), BF16),
            pltpu.SemaphoreType.DMA((4,)),
            pltpu.SemaphoreType.DMA((copies,)),
        ],
    )(info, normed_t, grad, upper, context)


def bit_orders(count):
    bits = [1 << b for b in range(count.bit_length() - 1)]
    if len(bits) < 3:
        return [bits] * 3
    near, far = bits[:3], bits[3:]
    return [far + near[c:] + near[:c] for c in range(3)]


def slot_offsets(order):
    offsets = [0]
    for bit in order:
        offsets = offsets + [offset ^ bit for offset in offsets]
    return offsets


def across(value, bit):
    count = lax.axis_size("dp")
    return lax.ppermute(value, "dp", [(source, source ^ bit) for source in range(count)])


def gather_rows(shard, orders, columns):
    held = [shard[None, :, start:stop] for start, stop in columns]
    final = [None] * len(columns)
    steps = len(orders[0])
    for step in range(steps):
        got = [across(held[c], orders[c][step]) for c in range(len(columns))]
        for c in range(len(columns)):
            if step + 1 == steps:
                final[c] = (held[c], got[c])
            else:
                held[c] = jnp.concatenate([held[c], got[c]], axis=0)
    return final


def scatter_rows(terms, orders, scale):
    chunk_count = len(orders)
    steps = len(orders[0])
    kept = [[terms[2 * c]] for c in range(chunk_count)]
    outgoing = [terms[2 * c + 1] for c in range(chunk_count)]
    for step in reversed(range(steps)):
        got = [across(outgoing[c], orders[c][step]) for c in range(chunk_count)]
        for c in range(chunk_count):
            kept[c].append(got[c])
        if step:
            half = 1 << (step - 1)
            for c in range(chunk_count):
                total = sum(part[half : 2 * half].astype(F32) for part in kept[c])
                outgoing[c] = total.astype(BF16)
    sums = [sum(part[0].astype(F32) for part in kept[c]) * scale for c in range(chunk_count)]
    return jnp.concatenate(sums, axis=-1)


def on_device(layer_input, saved_qkv, ln_gain, layer_weights, rand_blocks, out_grad):
    sections = lax.axis_size("pipe")
    section = lax.axis_index("pipe")
    replicas = lax.axis_size("dp")
    position = lax.axis_index("dp")
    x, qkv, top, shard = layer_input[0, 0], saved_qkv[0, 0], out_grad[0], layer_weights[0]
    rows, total = shard.shape
    orders = bit_orders(replicas)
    chunk = total // len(orders)
    columns = [(c * chunk, (c + 1) * chunk) for c in range(len(orders))]
    layout = ([slot_offsets(order) for order in orders], columns)

    gathered = gather_rows(shard, orders, columns)

    blocks = x.shape[0] // BLOCK
    draws = jnp.sum(rand_blocks[0], axis=-1)
    low_all = sum(range(3, blocks - 1))
    high_all = sum(range(1, blocks - 3))
    skipped = jnp.stack([low_all - draws[:, 0], high_all - draws[:, -1]])
    weights, context = attend_forward(qkv, skipped)
    normed_t = normed_transposed(x, ln_gain)

    is_top = (section == sections - 1).astype(jnp.int32)
    received = top
    carry = grad_input = None
    for turn in range(sections):
        active = (section == sections - 1 - turn).astype(jnp.int32)
        info = jnp.stack([active, is_top, position])
        carry = attend_backward(
            info, received, top, qkv, weights, context, gathered, layout, carry
        )
        if turn + 1 < sections:
            grad_input = project(
                info, ln_gain, carry[1], carry[0], x, gathered, layout, grad_input
            )
            received = lax.ppermute(
                grad_input, "pipe", [(source, source - 1) for source in range(1, sections)]
            )
    grad, upper = carry
    terms = weight_terms(info, normed_t, grad, upper, context, rows, layout)
    summed = scatter_rows(terms, orders, 1.0 / replicas)
    grad_input = project(info, ln_gain, upper, grad, x, gathered, layout, grad_input)
    return (grad_input[None, None], summed[None])


def solution(mesh):
    placed = (
        P("pipe", "dp", None, None),
        P("pipe", "dp", None, None),
        P("pipe", None),
        P("pipe", "dp", None),
        P("pipe", None, None, None),
        P("dp", None, None),
    )
    return jax.shard_map(
        on_device,
        mesh=mesh,
        in_specs=placed,
        out_specs=(P("pipe", "dp", None, None), P("pipe", "dp", None)),
        check_vma=False,
    )
```

time: 890 us -> 149 us (0.17); the launches traced: 877 us -> 148 us
  waiting for transfers between devices: 453 us -> 57.2 us
  other arithmetic: 173 us -> 4.13 us
  local copies, waits for them, and re-layouts: 150 us -> 1.93 us
  matrix products: 74.7 us -> 0 us
  Pallas kernels: 0 us -> 47.4 us
  starting transfers between devices: 1.37 us -> 36.9 us
  between operations: 14.9 us -> 0.89 us
  loops' own time: 10.6 us -> 0 us
    ppermute x1 -> x25, waiting for transfers between devices: 272 us -> 57.2 us  [the longest x24 39.8 us: across(): lax.ppermute(value, 'dp', [(source, source ^ bit) for source in range(cou...]
    reduce_scatter x1 -> x0, waiting for transfers between devices: 171 us -> none  [on_device(): summed = lax.psum_scatter(term, 'dp', scatter_dimension=0, tiled=True)]
    scatter-add x2 -> x0, other arithmetic: 126 us -> none  [the longest x1 63.1 us: attend_backward(): key_grad = jnp.zeros(queries.shape, jnp.float32).at[head_index, key_table...]
    dot_general x16 -> x0, matrix products: 74.7 us -> none  [the longest x12 58.5 us: product(): return jnp.einsum(form, left, right, preferred_element_type=jnp.float32)]
    reshape x23 -> x0, local copies, waits for them, and re-layouts: 73.6 us -> none  [the longest x13 28.9 us: to_heads(): matrix.reshape(block_count, BLOCK, HEADS, HEAD_DIM).transpose(2, 0, 1, 3)]
    pallas_call x0 -> x7, Pallas kernels: none -> 47.4 us  [the longest x2 16.6 us: attend_backward(): call(body, (shape((length, 3 * INNER)), shape((length, width))), [SMEM] +...]
    gather x4 -> x0, local copies, waits for them, and re-layouts: 40.2 us -> none  [the longest x2 20.2 us: arrange(): keys_all[head_index, key_table]]
    ppermute x1 -> x25, starting transfers between devices: 1.29 us -> 36.9 us  [the longest x24 35.6 us: across(): lax.ppermute(value, 'dp', [(source, source ^ bit) for source in range(cou...]
  transfers between devices with their start and end apart: 3 -> 25, of which waited for: 3 -> 16; matrix products, arithmetic and copies ran while one was open for 10% -> 2% of each run, Pallas kernels for 0% -> 15%
where the time goes in v1:
time: 149 us; the launch traced here: 148 us
  waiting for transfers between devices  57.2 us (38%)
  Pallas kernels  47.4 us (32%)
  starting transfers between devices  36.9 us (25%)
  other arithmetic  4.13 us (3%)
  local copies, waits for them, and re-layouts  1.93 us (1%)
    ppermute x24, waiting for transfers between devices, across(): lax.ppermute(value, 'dp', [(source, source ^ bit) for source in range(cou...  39.8 us
    ppermute x24, starting transfers between devices, across(): lax.ppermute(value, 'dp', [(source, source ^ bit) for source in range(cou...  35.6 us
    ppermute x1, waiting for transfers between devices, on_device(): lax.ppermute(grad_input, 'pipe', [(source, source - 1) for source in rang...  17.4 us
    pallas_call x2, Pallas kernels, attend_backward(): call(body, (shape((length, 3 * INNER)), shape((length, width))), [SMEM] +...  16.6 us
    pallas_call x1, Pallas kernels, attend_forward(): pl.pallas_call(forward_body, grid_spec=pltpu.PrefetchScalarGridSpec(num_s...  11.3 us
    pallas_call x2, Pallas kernels, project(): call(body, shape((length, width)), [SMEM, pl.BlockSpec(memory_space=pltpu...  9 us
    pallas_call x1, Pallas kernels, weight_terms(): call(body, outs, [SMEM] + [ANY] * 4, (ANY,) * len(outs), [pltpu.VMEM((wid...  7.77 us
  transfers between devices with their start and end apart: 25, of which 16 were waited for; matrix products, arithmetic and copies ran while one was open for 2% of the time, Pallas kernels for 15%

profile of v1, /device:TPU:0, one launch (start us, length us, event | category | flops | bytes accessed | tf_op | source)
XLA Modules:
  0.0 148.4 jit_solution(3891716866271684808)
XLA Ops:
  0.6 1.0 slice_bitcast_fusion
  1.6 4.1 %collective-permute-start.8 = (bf16[1,48,1024]{2,1,0:T(8,128)(2,1)S(1)}, bf16[1,48,1024]{2,1,0:T(8,128)(2,1)S(1)}, u32[]{:S(2)}, u32[]{:S(2)}) collective-permute-start(bf16[1,48,1024]{2,1,0:T(8,128)(2,1)S(1)} %get-tuple-element.26), channel_id=1, source_target_pairs={{0,8},{1,9},{2,10},{3,11},{4,12},{5,13},{6,14},{7,15},{8,0},{9,1},... | collective-permute-start | bytes 294920 | tf_op jit(solution)/shard_map/ppermute | solution.py:440
  5.8 2.8 %collective-permute-start.4 = (bf16[1,48,1024]{2,1,0:T(8,128)(2,1)S(1)}, bf16[1,48,1024]{2,1,0:T(8,128)(2,1)S(1)}, u32[]{:S(2)}, u32[]{:S(2)}) collective-permute-start(bf16[1,48,1024]{2,1,0:T(8,128)(2,1)S(1)} %get-tuple-element.27), channel_id=1, source_target_pairs={{0,8},{1,9},{2,10},{3,11},{4,12},{5,13},{6,14},{7,15},{8,0},{9,1},... | collective-permute-start | bytes 294920 | tf_op jit(solution)/shard_map/ppermute | solution.py:440
  8.7 7.0 %collective-permute-done.8 = bf16[1,48,1024]{2,1,0:T(8,128)(2,1)S(1)} collective-permute-done((bf16[1,48,1024]{2,1,0:T(8,128)(2,1)S(1)}, bf16[1,48,1024]{2,1,0:T(8,128)(2,1)S(1)}, u32[]{:S(2)}, u32[]{:S(2)}) %collective-permute-start.8) | collective-permute-done | bytes 98336 | tf_op jit(solution)/shard_map/ppermute | solution.py:440
  15.8 2.1 %collective-permute-done = bf16[1,48,1024]{2,1,0:T(8,128)(2,1)S(1)} collective-permute-done((bf16[1,48,1024]{2,1,0:T(8,128)(2,1)S(1)}, bf16[1,48,1024]{2,1,0:T(8,128)(2,1)S(1)}, u32[]{:S(2)}, u32[]{:S(2)}) %collective-permute-start) | collective-permute-done | bytes 98336 | tf_op jit(solution)/shard_map/ppermute | solution.py:440
  17.9 1.8 %collective-permute-start.1 = (bf16[2,48,1024]{2,1,0:T(8,128)(2,1)S(1)}, bf16[2,48,1024]{2,1,0:T(8,128)(2,1)S(1)}, u32[]{:S(2)}, u32[]{:S(2)}) collective-permute-start(bf16[2,48,1024]{2,1,0:T(8,128)(2,1)S(1)} %pad_maximum_fusion.6), channel_id=1, source_target_pairs={{0,1},{1,0},{2,3},{3,2},{4,5},{5,4},{6,7},{7,6},{8,9},{9,8},{10,11... | collective-permute-start | bytes 589832 | tf_op jit(solution)/shard_map/ppermute | solution.py:440
  19.7 1.6 %collective-permute-start.5 = (bf16[2,48,1024]{2,1,0:T(8,128)(2,1)S(1)}, bf16[2,48,1024]{2,1,0:T(8,128)(2,1)S(1)}, u32[]{:S(2)}, u32[]{:S(2)}) collective-permute-start(bf16[2,48,1024]{2,1,0:T(8,128)(2,1)S(1)} %pad_maximum_fusion.7), channel_id=1, source_target_pairs={{0,2},{1,3},{2,0},{3,1},{4,6},{5,7},{6,4},{7,5},{8,10},{9,11},{10,... | collective-permute-start | bytes 589832 | tf_op jit(solution)/shard_map/ppermute | solution.py:440
  21.3 2.0 %collective-permute-done.9 = bf16[2,48,1024]{2,1,0:T(8,128)(2,1)S(1)} collective-permute-done((bf16[2,48,1024]{2,1,0:T(8,128)(2,1)S(1)}, bf16[2,48,1024]{2,1,0:T(8,128)(2,1)S(1)}, u32[]{:S(2)}, u32[]{:S(2)}) %collective-permute-start.9) | collective-permute-done | bytes 196640 | tf_op jit(solution)/shard_map/ppermute | solution.py:440
  23.3 1.6 %collective-permute-start.10 = (bf16[4,48,1024]{2,1,0:T(8,128)(2,1)S(1)}, bf16[4,48,1024]{2,1,0:T(8,128)(2,1)S(1)}, u32[]{:S(2)}, u32[]{:S(2)}) collective-permute-start(bf16[4,48,1024]{2,1,0:T(8,128)(2,1)S(1)} %pad_maximum_fusion.5), channel_id=1, source_target_pairs={{0,1},{1,0},{2,3},{3,2},{4,5},{5,4},{6,7},{7,6},{8,9},{9,8},{10,11... | collective-permute-start | bytes 1179656 | tf_op jit(solution)/shard_map/ppermute | solution.py:440
  25.0 1.6 %collective-permute-start.2 = (bf16[4,48,1024]{2,1,0:T(8,128)(2,1)S(1)}, bf16[4,48,1024]{2,1,0:T(8,128)(2,1)S(1)}, u32[]{:S(2)}, u32[]{:S(2)}) collective-permute-start(bf16[4,48,1024]{2,1,0:T(8,128)(2,1)S(1)} %pad_maximum_fusion.3), channel_id=1, source_target_pairs={{0,2},{1,3},{2,0},{3,1},{4,6},{5,7},{6,4},{7,5},{8,10},{9,11},{10,... | collective-permute-start | bytes 1179656 | tf_op jit(solution)/shard_map/ppermute | solution.py:440
  26.9 7.3 %collective-permute-done.10 = bf16[4,48,1024]{2,1,0:T(8,128)(2,1)S(1)} collective-permute-done((bf16[4,48,1024]{2,1,0:T(8,128)(2,1)S(1)}, bf16[4,48,1024]{2,1,0:T(8,128)(2,1)S(1)}, u32[]{:S(2)}, u32[]{:S(2)}) %collective-permute-start.10) | collective-permute-done | bytes 393248 | tf_op jit(solution)/shard_map/ppermute | solution.py:440
  34.4 1.4 collective-permute-start.11
  35.9 0.8 collective-permute-done.6
  36.9 0.7 collective-permute-start.7
  37.6 0.6 pad_add_fusion.skip_ref
  38.2 11.3 %shard_map.77 = (bf16[12,512,512]{2,1,0:T(8,128)(2,1)}, bf16[512,768]{1,0:T(8,128)(2,1)}) custom-call(s32[2,12]{1,0:T(2,128)} %pad_add_fusion.skip_ref, bf16[512,2304]{1,0:T(8,128)(2,1)} %bitcast.26, bf16[512,2304]{1,0:T(8,128)(2,1)} %bitcast.27, bf16[512,2304]{1,0:T(8,128)(2,1)} %bitcast.28), custom_call_target="tpu_custom_call" | custom-call | tf_op jit(solution)/shard_map/pallas_call | solution.py:89
  49.6 0.6 add_add_fusion.1.refs_0_
  50.2 2.7 %collective-permute-done.11.refs_11_.refs_10_ = bf16[8,48,1024]{2,1,0:T(8,128)(2,1)S(1)} collective-permute-done((bf16[8,48,1024]{2,1,0:T(8,128)(2,1)S(1)}, bf16[8,48,1024]{2,1,0:T(8,128)(2,1)S(1)}, u32[]{:S(2)}, u32[]{:S(2)}) %collective-permute-start.11) | collective-permute-done | bytes 786464 | tf_op jit(solution)/shard_map/ppermute | solution.py:440
  52.8 1.1 collective-permute-done.3.refs_7_.refs_6_
  53.9 0.7 collective-permute-done.7.refs_9_.refs_8_
  54.6 0.9 shard_map.78
  55.5 1.2 shard_map.79.refs_11_
  56.7 1.3 collective-permute-start.12
  58.0 2.7 %shard_map.82.refs_1_ = bf16[768,512]{1,0:T(8,128)(2,1)} custom-call(bf16[512,768]{1,0:T(8,128)(2,1)} %bitcast.35, f32[1,768]{1,0:T(1,128)} %gain_ref.1), custom_call_target="tpu_custom_call" | custom-call | tf_op jit(solution)/shard_map/pallas_call | solution.py:123
  60.7 0.6 add_add_fusion.refs_0_
  61.3 17.4 %collective-permute-done.12.refs_1_ = bf16[512,768]{1,0:T(8,128)(2,1)S(1)} collective-permute-done((bf16[512,768]{1,0:T(8,128)(2,1)}, bf16[512,768]{1,0:T(8,128)(2,1)S(1)}, u32[]{:S(2)}, u32[]{:S(2)}) %collective-permute-start.12) | collective-permute-done | bytes 786464 | tf_op jit(solution)/shard_map/ppermute | solution.py:510
  78.7 0.9 copy-done.4
  79.6 15.7 %shard_map.80 = (bf16[512,2304]{1,0:T(8,128)(2,1)}, bf16[512,768]{1,0:T(8,128)(2,1)}) custom-call(s32[3]{0:T(128)} %add_add_fusion.refs_0_, bf16[512,768]{1,0:T(8,128)(2,1)} %copy-done.4, bf16[512,768]{1,0:T(8,128)(2,1)} %bitcast.33, bf16[512,2304]{1,0:T(8,128)(2,1)} %bitcast.30, ...), custom_call_target="tpu_custom_call", output_to_operand_aliasing={{0}: (12, {}), {1}: (13, {})} | custom-call | tf_op jit(solution)/shard_map/pallas_call | solution.py:257
  95.3 7.8 %shard_map.83 = (bf16[8,48,1024]{2,1,0:T(8,128)(2,1)}, bf16[8,48,1024]{2,1,0:T(8,128)(2,1)}, bf16[8,48,1024]{2,1,0:T(8,128)(2,1)}, bf16[8,48,1024]{2,1,0:T(8,128...) custom-call(s32[3]{0:T(128)} %add_add_fusion.refs_0_, bf16[768,512]{1,0:T(8,128)(2,1)} %shard_map.82.refs_1_, ...), custom_call_target="tpu_custom_call" | custom-call | tf_op jit(solution)/shard_map/pallas_call | solution.py:406
  103.1 1.2 collective-permute-start.13
  104.3 1.5 %collective-permute-start.17 = (bf16[8,48,1024]{2,1,0:T(8,128)(2,1)}, bf16[8,48,1024]{2,1,0:T(8,128)(2,1)S(1)}, u32[]{:S(2)}, u32[]{:S(2)}) collective-permute-start(bf16[8,48,1024]{2,1,0:T(8,128)(2,1)} %get-tuple-element.23), channel_id=1, source_target_pairs={{0,1},{1,0},{2,3},{3,2},{4,5},{5,4},{6,7},{7,6},{8,9},{9,8},{10,11... | collective-permute-start | bytes 2359304 | tf_op jit(solution)/shard_map/ppermute | solution.py:440
  105.8 0.7 collective-permute-start.21
  106.4 7.8 %shard_map.81 = bf16[512,768]{1,0:T(8,128)(2,1)} custom-call(s32[3]{0:T(128)} %add_add_fusion.refs_0_, f32[1,768]{1,0:T(1,128)} %gain_ref.1, bf16[512,768]{1,0:T(8,128)(2,1)} %get-tuple-element.18.refs_2_.refs_3_, bf16[512,2304]{1,0:T(8,128)(2,1)} %get-tuple-element.19.refs_3_.refs_2_, bf16[512,768]{1,0:T(8,128)(2,1)} %bitcast.36, ...), custom_call_target="tpu_custom_call", output_to_operand_aliasing={{}: (11, {})} | custom-call | tf_op jit(solution)/shard_map/pallas_call | solution.py:324
  114.3 5.1 %collective-permute-done.13 = bf16[8,48,1024]{2,1,0:T(8,128)(2,1)S(1)} collective-permute-done((bf16[8,48,1024]{2,1,0:T(8,128)(2,1)}, bf16[8,48,1024]{2,1,0:T(8,128)(2,1)S(1)}, u32[]{:S(2)}, u32[]{:S(2)}) %collective-permute-start.13) | collective-permute-done | bytes 786464 | tf_op jit(solution)/shard_map/ppermute | solution.py:440
  119.5 1.2 collective-permute-start.14
  120.9 1.2 collective-permute-start.18
  122.2 1.6 %collective-permute-start.22 = (bf16[4,48,1024]{2,1,0:T(8,128)(2,1)S(1)}, bf16[4,48,1024]{2,1,0:T(8,128)(2,1)S(1)}, u32[]{:S(2)}, u32[]{:S(2)}) collective-permute-start(bf16[4,48,1024]{2,1,0:T(8,128)(2,1)S(1)} %add_convert_fusion), channel_id=1, source_target_pairs={{0,1},{1,0},{2,3},{3,2},{4,5},{5,4},{6,7},{7,6},{8,9},{9,8},{10,11... | collective-permute-start | bytes 1179656 | tf_op jit(solution)/shard_map/ppermute | solution.py:440
  123.8 3.6 %collective-permute-done.14 = bf16[4,48,1024]{2,1,0:T(8,128)(2,1)S(1)} collective-permute-done((bf16[4,48,1024]{2,1,0:T(8,128)(2,1)S(1)}, bf16[4,48,1024]{2,1,0:T(8,128)(2,1)S(1)}, u32[]{:S(2)}, u32[]{:S(2)}) %collective-permute-start.14) | collective-permute-done | bytes 393248 | tf_op jit(solution)/shard_map/ppermute | solution.py:440
  127.5 1.6 %collective-permute-start.15 = (bf16[2,48,1024]{2,1,0:T(8,128)(2,1)S(1)}, bf16[2,48,1024]{2,1,0:T(8,128)(2,1)S(1)}, u32[]{:S(2)}, u32[]{:S(2)}) collective-permute-start(bf16[2,48,1024]{2,1,0:T(8,128)(2,1)S(1)} %add_convert_fusion.5), channel_id=1, source_target_pairs={{0,1},{1,0},{2,3},{3,2},{4,5},{5,4},{6,7},{7,6},{8,9},{9,8},{10,11... | collective-permute-start | bytes 589832 | tf_op jit(solution)/shard_map/ppermute | solution.py:440
  129.0 1.6 %collective-permute-done.18 = bf16[4,48,1024]{2,1,0:T(8,128)(2,1)S(1)} collective-permute-done((bf16[4,48,1024]{2,1,0:T(8,128)(2,1)S(1)}, bf16[4,48,1024]{2,1,0:T(8,128)(2,1)S(1)}, u32[]{:S(2)}, u32[]{:S(2)}) %collective-permute-start.18) | collective-permute-done | bytes 393248 | tf_op jit(solution)/shard_map/ppermute | solution.py:440
  130.7 1.1 collective-permute-start.19
  131.9 1.0 collective-permute-start.23
  133.3 5.4 %collective-permute-start.16 = (bf16[1,48,1024]{2,1,0:T(8,128)(2,1)S(1)}, bf16[1,48,1024]{2,1,0:T(8,128)(2,1)S(1)}, u32[]{:S(2)}, u32[]{:S(2)}) collective-permute-start(bf16[1,48,1024]{2,1,0:T(8,128)(2,1)S(1)} %add_convert_fusion.8), channel_id=1, source_target_pairs={{0,8},{1,9},{2,10},{3,11},{4,12},{5,13},{6,14},{7,15},{8,0},{9,1},... | collective-permute-start | bytes 294920 | tf_op jit(solution)/shard_map/ppermute | solution.py:440
  138.7 0.8 collective-permute-start.20
  139.6 2.2 %collective-permute-start.24 = (bf16[1,48,1024]{2,1,0:T(8,128)(2,1)S(1)}, bf16[1,48,1024]{2,1,0:T(8,128)(2,1)S(1)}, u32[]{:S(2)}, u32[]{:S(2)}) collective-permute-start(bf16[1,48,1024]{2,1,0:T(8,128)(2,1)S(1)} %add_convert_fusion.6), channel_id=1, source_target_pairs={{0,8},{1,9},{2,10},{3,11},{4,12},{5,13},{6,14},{7,15},{8,0},{9,1},... | collective-permute-start | bytes 294920 | tf_op jit(solution)/shard_map/ppermute | solution.py:440
  142.4 3.0 %collective-permute-done.20 = bf16[1,48,1024]{2,1,0:T(8,128)(2,1)S(1)} collective-permute-done((bf16[1,48,1024]{2,1,0:T(8,128)(2,1)S(1)}, bf16[1,48,1024]{2,1,0:T(8,128)(2,1)S(1)}, u32[]{:S(2)}, u32[]{:S(2)}) %collective-permute-start.20) | collective-permute-done | bytes 98336 | tf_op jit(solution)/shard_map/ppermute | solution.py:440
  145.4 2.0 %collective-permute-done.24 = bf16[1,48,1024]{2,1,0:T(8,128)(2,1)S(1)} collective-permute-done((bf16[1,48,1024]{2,1,0:T(8,128)(2,1)S(1)}, bf16[1,48,1024]{2,1,0:T(8,128)(2,1)S(1)}, u32[]{:S(2)}, u32[]{:S(2)}) %collective-permute-start.24) | collective-permute-done | bytes 98336 | tf_op jit(solution)/shard_map/ppermute | solution.py:440
  147.5 0.9 maximum_bitcast_fusion
  (55 shorter events, 2.8 us)
Async XLA Ops:
  1.6 14.0 %collective-permute-start.8 = (bf16[1,48,1024]{2,1,0:T(8,128)(2,1)S(1)}, bf16[1,48,1024]{2,1,0:T(8,128)(2,1)S(1)}, u32[]{:S(2)}, u32[]{:S(2)}) collective-permute-start(bf16[1,48,1024]{2,1,0:T(8,128)(2,1)S(1)} %get-tuple-element.26), channel_id=1, source_target_pairs={{0,8},{1,9},{2,10},{3,11},{4,12},{5,13},{6,14},{7,15},{8,0},{9,1},... | collective-permute-start | bytes 294920 | tf_op jit(solution)/shard_map/ppermute | solution.py:440
  5.7 12.1 %collective-permute-start = (bf16[1,48,1024]{2,1,0:T(8,128)(2,1)S(1)}, bf16[1,48,1024]{2,1,0:T(8,128)(2,1)S(1)}, u32[]{:S(2)}, u32[]{:S(2)}) collective-permute-start(bf16[1,48,1024]{2,1,0:T(8,128)(2,1)S(1)} %get-tuple-element.28), channel_id=1, source_target_pairs={{0,8},{1,9},{2,10},{3,11},{4,12},{5,13},{6,14},{7,15},{8,0},{9,1},... | collective-permute-start | bytes 294920 | tf_op jit(solution)/shard_map/ppermute | solution.py:440
  5.8 13.9 %collective-permute-start.4 = (bf16[1,48,1024]{2,1,0:T(8,128)(2,1)S(1)}, bf16[1,48,1024]{2,1,0:T(8,128)(2,1)S(1)}, u32[]{:S(2)}, u32[]{:S(2)}) collective-permute-start(bf16[1,48,1024]{2,1,0:T(8,128)(2,1)S(1)} %get-tuple-element.27), channel_id=1, source_target_pairs={{0,8},{1,9},{2,10},{3,11},{4,12},{5,13},{6,14},{7,15},{8,0},{9,1},... | collective-permute-start | bytes 294920 | tf_op jit(solution)/shard_map/ppermute | solution.py:440
  15.7 7.6 %collective-permute-start.9 = (bf16[2,48,1024]{2,1,0:T(8,128)(2,1)S(1)}, bf16[2,48,1024]{2,1,0:T(8,128)(2,1)S(1)}, u32[]{:S(2)}, u32[]{:S(2)}) collective-permute-start(bf16[2,48,1024]{2,1,0:T(8,128)(2,1)S(1)} %pad_maximum_fusion.8), channel_id=1, source_target_pairs={{0,4},{1,5},{2,6},{3,7},{4,0},{5,1},{6,2},{7,3},{8,12},{9,13},{10,... | collective-permute-start | bytes 589832 | tf_op jit(solution)/shard_map/ppermute | solution.py:440
  17.9 7.0 %collective-permute-start.1 = (bf16[2,48,1024]{2,1,0:T(8,128)(2,1)S(1)}, bf16[2,48,1024]{2,1,0:T(8,128)(2,1)S(1)}, u32[]{:S(2)}, u32[]{:S(2)}) collective-permute-start(bf16[2,48,1024]{2,1,0:T(8,128)(2,1)S(1)} %pad_maximum_fusion.6), channel_id=1, source_target_pairs={{0,1},{1,0},{2,3},{3,2},{4,5},{5,4},{6,7},{7,6},{8,9},{9,8},{10,11... | collective-permute-start | bytes 589832 | tf_op jit(solution)/shard_map/ppermute | solution.py:440
  19.7 6.9 %collective-permute-start.5 = (bf16[2,48,1024]{2,1,0:T(8,128)(2,1)S(1)}, bf16[2,48,1024]{2,1,0:T(8,128)(2,1)S(1)}, u32[]{:S(2)}, u32[]{:S(2)}) collective-permute-start(bf16[2,48,1024]{2,1,0:T(8,128)(2,1)S(1)} %pad_maximum_fusion.7), channel_id=1, source_target_pairs={{0,2},{1,3},{2,0},{3,1},{4,6},{5,7},{6,4},{7,5},{8,10},{9,11},{10,... | collective-permute-start | bytes 589832 | tf_op jit(solution)/shard_map/ppermute | solution.py:440
  23.3 10.9 %collective-permute-start.10 = (bf16[4,48,1024]{2,1,0:T(8,128)(2,1)S(1)}, bf16[4,48,1024]{2,1,0:T(8,128)(2,1)S(1)}, u32[]{:S(2)}, u32[]{:S(2)}) collective-permute-start(bf16[4,48,1024]{2,1,0:T(8,128)(2,1)S(1)} %pad_maximum_fusion.5), channel_id=1, source_target_pairs={{0,1},{1,0},{2,3},{3,2},{4,5},{5,4},{6,7},{7,6},{8,9},{9,8},{10,11... | collective-permute-start | bytes 1179656 | tf_op jit(solution)/shard_map/ppermute | solution.py:440
  25.0 10.8 %collective-permute-start.2 = (bf16[4,48,1024]{2,1,0:T(8,128)(2,1)S(1)}, bf16[4,48,1024]{2,1,0:T(8,128)(2,1)S(1)}, u32[]{:S(2)}, u32[]{:S(2)}) collective-permute-start(bf16[4,48,1024]{2,1,0:T(8,128)(2,1)S(1)} %pad_maximum_fusion.3), channel_id=1, source_target_pairs={{0,2},{1,3},{2,0},{3,1},{4,6},{5,7},{6,4},{7,5},{8,10},{9,11},{10,... | collective-permute-start | bytes 1179656 | tf_op jit(solution)/shard_map/ppermute | solution.py:440
  26.6 11.0 %copy-start.8 = (s32[1,12,6,3]{1,0,3,2:T(1,128)S(1)}, s32[1,12,6,3]{1,0,3,2:T(1,128)}, u32[]{:S(2)}) copy-start(s32[1,12,6,3]{1,0,3,2:T(1,128)} %param.10) | copy-start | bytes 2596
  26.6 10.1 %collective-permute-start.6 = (bf16[4,48,1024]{2,1,0:T(8,128)(2,1)S(1)}, bf16[4,48,1024]{2,1,0:T(8,128)(2,1)S(1)}, u32[]{:S(2)}, u32[]{:S(2)}) collective-permute-start(bf16[4,48,1024]{2,1,0:T(8,128)(2,1)S(1)} %pad_maximum_fusion.4), channel_id=1, source_target_pairs={{0,4},{1,5},{2,6},{3,7},{4,0},{5,1},{6,2},{7,3},{8,12},{9,13},{10,... | collective-permute-start | bytes 1179656 | tf_op jit(solution)/shard_map/ppermute | solution.py:440
  34.3 15.2 %copy-start = (bf16[8,48,1024]{2,1,0:T(8,128)(2,1)}, bf16[8,48,1024]{2,1,0:T(8,128)(2,1)S(1)}, u32[]{:S(2)}) copy-start(bf16[8,48,1024]{2,1,0:T(8,128)(2,1)S(1)} %pad_maximum_fusion.2.refs_10_.refs_9_) | copy-start | bytes 2359300
  34.4 18.5 %collective-permute-start.11 = (bf16[8,48,1024]{2,1,0:T(8,128)(2,1)S(1)}, bf16[8,48,1024]{2,1,0:T(8,128)(2,1)S(1)}, u32[]{:S(2)}, u32[]{:S(2)}) collective-permute-start(bf16[8,48,1024]{2,1,0:T(8,128)(2,1)S(1)} %pad_maximum_fusion.2.refs_10_.refs_9_), channel_id=1, source_target_pairs={{0,2},{1,3},{2,0},{3,1},{4,6},{5,7},{6,4},{7,5},{8,10},{9,11},{10,... | collective-permute-start | bytes 2359304 | tf_op jit(solution)/shard_map/ppermute | solution.py:440
  35.8 13.7 %copy-start.1 = (bf16[8,48,1024]{2,1,0:T(8,128)(2,1)}, bf16[8,48,1024]{2,1,0:T(8,128)(2,1)S(1)}, u32[]{:S(2)}) copy-start(bf16[8,48,1024]{2,1,0:T(8,128)(2,1)S(1)} %pad_maximum_fusion.refs_6_.refs_5_) | copy-start | bytes 2359300
  35.9 18.0 %collective-permute-start.3 = (bf16[8,48,1024]{2,1,0:T(8,128)(2,1)S(1)}, bf16[8,48,1024]{2,1,0:T(8,128)(2,1)}, u32[]{:S(2)}, u32[]{:S(2)}) collective-permute-start(bf16[8,48,1024]{2,1,0:T(8,128)(2,1)S(1)} %pad_maximum_fusion.refs_6_.refs_5_), channel_id=1, source_target_pairs={{0,4},{1,5},{2,6},{3,7},{4,0},{5,1},{6,2},{7,3},{8,12},{9,13},{10,... | collective-permute-start | bytes 2359304 | tf_op jit(solution)/shard_map/ppermute | solution.py:440
  36.9 12.7 %copy-start.2 = (bf16[8,48,1024]{2,1,0:T(8,128)(2,1)}, bf16[8,48,1024]{2,1,0:T(8,128)(2,1)S(1)}, u32[]{:S(2)}) copy-start(bf16[8,48,1024]{2,1,0:T(8,128)(2,1)S(1)} %pad_maximum_fusion.1.refs_8_.refs_7_) | copy-start | bytes 2359300
  36.9 17.8 %collective-permute-start.7 = (bf16[8,48,1024]{2,1,0:T(8,128)(2,1)S(1)}, bf16[8,48,1024]{2,1,0:T(8,128)(2,1)}, u32[]{:S(2)}, u32[]{:S(2)}) collective-permute-start(bf16[8,48,1024]{2,1,0:T(8,128)(2,1)S(1)} %pad_maximum_fusion.1.refs_8_.refs_7_), channel_id=1, source_target_pairs={{0,1},{1,0},{2,3},{3,2},{4,5},{5,4},{6,7},{7,6},{8,9},{9,8},{10,11... | collective-permute-start | bytes 2359304 | tf_op jit(solution)/shard_map/ppermute | solution.py:440
  52.8 1.8 %copy-start.3 = (bf16[8,48,1024]{2,1,0:T(8,128)(2,1)}, bf16[8,48,1024]{2,1,0:T(8,128)(2,1)S(1)}, u32[]{:S(2)}) copy-start(bf16[8,48,1024]{2,1,0:T(8,128)(2,1)S(1)} %collective-permute-done.11.refs_11_.refs_10_) | copy-start | bytes 2359300
  56.7 22.0 %collective-permute-start.12 = (bf16[512,768]{1,0:T(8,128)(2,1)}, bf16[512,768]{1,0:T(8,128)(2,1)S(1)}, u32[]{:S(2)}, u32[]{:S(2)}) collective-permute-start(bf16[512,768]{1,0:T(8,128)(2,1)} %shard_map.79.refs_11_), channel_id=1, source_target_pairs={{16,0},{17,1},{18,2},{19,3},{20,4},{21,5},{22,6},{23,7},{24,8},{25... | collective-permute-start | bytes 2359304 | tf_op jit(solution)/shard_map/ppermute | solution.py:510
  78.7 0.9 copy-start.4
  103.1 16.3 %collective-permute-start.13 = (bf16[8,48,1024]{2,1,0:T(8,128)(2,1)}, bf16[8,48,1024]{2,1,0:T(8,128)(2,1)S(1)}, u32[]{:S(2)}, u32[]{:S(2)}) collective-permute-start(bf16[8,48,1024]{2,1,0:T(8,128)(2,1)} %get-tuple-element.21), channel_id=1, source_target_pairs={{0,4},{1,5},{2,6},{3,7},{4,0},{5,1},{6,2},{7,3},{8,12},{9,13},{10,... | collective-permute-start | bytes 2359304 | tf_op jit(solution)/shard_map/ppermute | solution.py:440
  104.3 16.5 %collective-permute-start.17 = (bf16[8,48,1024]{2,1,0:T(8,128)(2,1)}, bf16[8,48,1024]{2,1,0:T(8,128)(2,1)S(1)}, u32[]{:S(2)}, u32[]{:S(2)}) collective-permute-start(bf16[8,48,1024]{2,1,0:T(8,128)(2,1)} %get-tuple-element.23), channel_id=1, source_target_pairs={{0,1},{1,0},{2,3},{3,2},{4,5},{5,4},{6,7},{7,6},{8,9},{9,8},{10,11... | collective-permute-start | bytes 2359304 | tf_op jit(solution)/shard_map/ppermute | solution.py:440
  105.8 13.6 %copy-start.7 = (bf16[8,48,1024]{2,1,0:T(8,128)(2,1)S(1)}, bf16[8,48,1024]{2,1,0:T(8,128)(2,1)}, u32[]{:S(2)}) copy-start(bf16[8,48,1024]{2,1,0:T(8,128)(2,1)} %get-tuple-element.20) | copy-start | bytes 2359300
  105.8 15.0 %copy-start.6 = (bf16[8,48,1024]{2,1,0:T(8,128)(2,1)S(1)}, bf16[8,48,1024]{2,1,0:T(8,128)(2,1)}, u32[]{:S(2)}) copy-start(bf16[8,48,1024]{2,1,0:T(8,128)(2,1)} %get-tuple-element.22) | copy-start | bytes 2359300
  105.8 16.3 %collective-permute-start.21 = (bf16[8,48,1024]{2,1,0:T(8,128)(2,1)}, bf16[8,48,1024]{2,1,0:T(8,128)(2,1)S(1)}, u32[]{:S(2)}, u32[]{:S(2)}) collective-permute-start(bf16[8,48,1024]{2,1,0:T(8,128)(2,1)} %get-tuple-element.25), channel_id=1, source_target_pairs={{0,2},{1,3},{2,0},{3,1},{4,6},{5,7},{6,4},{7,5},{8,10},{9,11},{10,... | collective-permute-start | bytes 2359304 | tf_op jit(solution)/shard_map/ppermute | solution.py:440
  114.3 7.8 %copy-start.5 = (bf16[8,48,1024]{2,1,0:T(8,128)(2,1)S(1)}, bf16[8,48,1024]{2,1,0:T(8,128)(2,1)}, u32[]{:S(2)}) copy-start(bf16[8,48,1024]{2,1,0:T(8,128)(2,1)} %get-tuple-element.24) | copy-start | bytes 2359300
  119.5 7.8 %collective-permute-start.14 = (bf16[4,48,1024]{2,1,0:T(8,128)(2,1)S(1)}, bf16[4,48,1024]{2,1,0:T(8,128)(2,1)S(1)}, u32[]{:S(2)}, u32[]{:S(2)}) collective-permute-start(bf16[4,48,1024]{2,1,0:T(8,128)(2,1)S(1)} %add_convert_fusion.2), channel_id=1, source_target_pairs={{0,2},{1,3},{2,0},{3,1},{4,6},{5,7},{6,4},{7,5},{8,10},{9,11},{10,... | collective-permute-start | bytes 1179656 | tf_op jit(solution)/shard_map/ppermute | solution.py:440
  120.9 9.8 %collective-permute-start.18 = (bf16[4,48,1024]{2,1,0:T(8,128)(2,1)S(1)}, bf16[4,48,1024]{2,1,0:T(8,128)(2,1)S(1)}, u32[]{:S(2)}, u32[]{:S(2)}) collective-permute-start(bf16[4,48,1024]{2,1,0:T(8,128)(2,1)S(1)} %add_convert_fusion.1), channel_id=1, source_target_pairs={{0,4},{1,5},{2,6},{3,7},{4,0},{5,1},{6,2},{7,3},{8,12},{9,13},{10,... | collective-permute-start | bytes 1179656 | tf_op jit(solution)/shard_map/ppermute | solution.py:440
  122.2 9.6 %collective-permute-start.22 = (bf16[4,48,1024]{2,1,0:T(8,128)(2,1)S(1)}, bf16[4,48,1024]{2,1,0:T(8,128)(2,1)S(1)}, u32[]{:S(2)}, u32[]{:S(2)}) collective-permute-start(bf16[4,48,1024]{2,1,0:T(8,128)(2,1)S(1)} %add_convert_fusion), channel_id=1, source_target_pairs={{0,1},{1,0},{2,3},{3,2},{4,5},{5,4},{6,7},{7,6},{8,9},{9,8},{10,11... | collective-permute-start | bytes 1179656 | tf_op jit(solution)/shard_map/ppermute | solution.py:440
  127.5 5.7 %collective-permute-start.15 = (bf16[2,48,1024]{2,1,0:T(8,128)(2,1)S(1)}, bf16[2,48,1024]{2,1,0:T(8,128)(2,1)S(1)}, u32[]{:S(2)}, u32[]{:S(2)}) collective-permute-start(bf16[2,48,1024]{2,1,0:T(8,128)(2,1)S(1)} %add_convert_fusion.5), channel_id=1, source_target_pairs={{0,1},{1,0},{2,3},{3,2},{4,5},{5,4},{6,7},{7,6},{8,9},{9,8},{10,11... | collective-permute-start | bytes 589832 | tf_op jit(solution)/shard_map/ppermute | solution.py:440
  130.7 7.9 %collective-permute-start.19 = (bf16[2,48,1024]{2,1,0:T(8,128)(2,1)S(1)}, bf16[2,48,1024]{2,1,0:T(8,128)(2,1)S(1)}, u32[]{:S(2)}, u32[]{:S(2)}) collective-permute-start(bf16[2,48,1024]{2,1,0:T(8,128)(2,1)S(1)} %add_convert_fusion.4), channel_id=1, source_target_pairs={{0,2},{1,3},{2,0},{3,1},{4,6},{5,7},{6,4},{7,5},{8,10},{9,11},{10,... | collective-permute-start | bytes 589832 | tf_op jit(solution)/shard_map/ppermute | solution.py:440
  131.9 7.6 %collective-permute-start.23 = (bf16[2,48,1024]{2,1,0:T(8,128)(2,1)S(1)}, bf16[2,48,1024]{2,1,0:T(8,128)(2,1)S(1)}, u32[]{:S(2)}, u32[]{:S(2)}) collective-permute-start(bf16[2,48,1024]{2,1,0:T(8,128)(2,1)S(1)} %add_convert_fusion.3), channel_id=1, source_target_pairs={{0,4},{1,5},{2,6},{3,7},{4,0},{5,1},{6,2},{7,3},{8,12},{9,13},{10,... | collective-permute-start | bytes 589832 | tf_op jit(solution)/shard_map/ppermute | solution.py:440
  133.3 9.0 %collective-permute-start.16 = (bf16[1,48,1024]{2,1,0:T(8,128)(2,1)S(1)}, bf16[1,48,1024]{2,1,0:T(8,128)(2,1)S(1)}, u32[]{:S(2)}, u32[]{:S(2)}) collective-permute-start(bf16[1,48,1024]{2,1,0:T(8,128)(2,1)S(1)} %add_convert_fusion.8), channel_id=1, source_target_pairs={{0,8},{1,9},{2,10},{3,11},{4,12},{5,13},{6,14},{7,15},{8,0},{9,1},... | collective-permute-start | bytes 294920 | tf_op jit(solution)/shard_map/ppermute | solution.py:440
  138.7 6.6 %collective-permute-start.20 = (bf16[1,48,1024]{2,1,0:T(8,128)(2,1)S(1)}, bf16[1,48,1024]{2,1,0:T(8,128)(2,1)S(1)}, u32[]{:S(2)}, u32[]{:S(2)}) collective-permute-start(bf16[1,48,1024]{2,1,0:T(8,128)(2,1)S(1)} %add_convert_fusion.7), channel_id=1, source_target_pairs={{0,8},{1,9},{2,10},{3,11},{4,12},{5,13},{6,14},{7,15},{8,0},{9,1},... | collective-permute-start | bytes 294920 | tf_op jit(solution)/shard_map/ppermute | solution.py:440
  139.6 7.9 %collective-permute-start.24 = (bf16[1,48,1024]{2,1,0:T(8,128)(2,1)S(1)}, bf16[1,48,1024]{2,1,0:T(8,128)(2,1)S(1)}, u32[]{:S(2)}, u32[]{:S(2)}) collective-permute-start(bf16[1,48,1024]{2,1,0:T(8,128)(2,1)S(1)} %add_convert_fusion.6), channel_id=1, source_target_pairs={{0,8},{1,9},{2,10},{3,11},{4,12},{5,13},{6,14},{7,15},{8,0},{9,1},... | collective-permute-start | bytes 294920 | tf_op jit(solution)/shard_map/ppermute | solution.py:440
